TPU v7x, 256 devices: a whole 4x4x8 slice. The times are simulated.
256 devices in a mesh: tile: 32 (over y, x, core), comp: 8 (over z).
Axes of the slice: x: 4, y: 4, z: 8, core: 2. Of those that a mesh axis runs over, the one named last changes fastest.
Arguments:
- spectrum: bfloat16 [768, 256, 1024], P('comp', 'tile'), may hold values from 0.049804688 to 2
- sea_mask: int32 [256, 1024], P('tile'), may hold values 0 or 1
- depth_class: int32 [256, 1024], P('tile'), may hold values from 0 to 15
- group_speed: float32 [16, 32], replicated, may hold values from 0.2 to 0.45
- wind_speed: float32 [256, 1024], P('tile'), may hold values from 2 to 20
- wind_dir: float32 [256, 1024], P('tile'), may hold values from -3.140625 to 3.140625
- coupling: bfloat16 [768, 768], replicated, may hold values from -0.21875 to 0.21875
Outputs:
- spectrum_next: bfloat16 [768, 256, 1024], P('comp', 'tile')
All inputs are finite; a program needn't handle non-finite values. No bound on the sum of `sea_mask` on one device may be relied on, other than what follows from the above.
Results may differ from a plain program's by a relative error of at most 0.002.
The roundings to bfloat16 on the way count: a program that leaves them out, or rounds other values in their place, can miss the bound.
Values may be sent and summed in bfloat16 or wider, within the bound.
A program may use at most 64 MiB of HBM per device.

v0:
```python
import functools
import math

import jax
import jax.numpy as jnp
import numpy as np
from jax import lax
from jax.experimental import pallas as pl
from jax.experimental.pallas import tpu as pltpu
from jax.sharding import PartitionSpec as P

K = 24
F = 32
DEPTHS = 16
PSTEPS = 4
SRC_STEPS = 4
COLS = 8
LANES = 128
GROUPS = 2
GCOLS = COLS // GROUPS
BF16 = jnp.bfloat16
F32 = jnp.float32


def tables():
    theta = np.arange(K).astype(np.float32) * np.float32(2.0 * math.pi / K)
    j = np.arange(F).astype(np.float64)
    rows = np.zeros((5, F), np.float32)
    rows[0, :K] = np.abs(np.cos(theta))
    rows[1, :K] = np.abs(np.sin(theta))
    rows[2] = 0.1 * 1.1**j
    rows[3] = 0.5 * 0.004 * 1.1 ** (j - 16.0)
    rows[4] = 0.5 * 0.3 * (j + 1.0) / F
    return rows


def step_kernel(
    parts, tiles,
    tab, table, sea_in, depth_in, wind_speed, wind_dir, spectrum, coupling_in, out,
    block, west, east, near_sea, near_depth, speed, sea, natural, sent, points, couple,
    state, nonlin, rounded, winds, back, turned,
    load_sem, couple_sem, mask_send, mask_recv, halo_send, halo_recv,
    out_send, out_recv, back_send, back_recv, own_sem,
):
    me = lax.axis_index("comp")
    tile = lax.axis_index("tile")
    left = lax.rem(tile + tiles - 1, tiles)
    right = lax.rem(tile + 1, tiles)
    comps, columns, rows = block.shape
    freqs = comps // K
    lane_tiles = rows // LANES
    groups = comps // 8
    per = K // 8
    far_first = sorted(range(1, parts), key=lambda d: -min(d, parts - d))

    def chunk_load(f):
        part = pl.ds(f * K, K)
        return pltpu.make_async_copy(spectrum.at[part], block.at[part], load_sem.at[f])

    def couple_load():
        return pltpu.make_async_copy(coupling_in, couple, couple_sem)

    for f in range(freqs):
        chunk_load(f).start()
    couple_load().start()

    barrier = pltpu.get_barrier_semaphore()
    for d in range(1, parts):
        pl.semaphore_signal(barrier, 1, device_id={"comp": lax.rem(me + d, parts)})
    for side in (left, right):
        pl.semaphore_signal(barrier, 1, device_id={"tile": side})
    pl.semaphore_wait(barrier, parts + 1)

    def mask_copy(side, target, array, which):
        return pltpu.make_async_remote_copy(
            (sea_in, depth_in)[array],
            (near_sea, near_depth)[array].at[side],
            mask_send.at[side, array], mask_recv.at[side, array],
            device_id={"tile": target},
        )

    def halo_copies(f):
        quarter = K // 4
        yield pltpu.make_async_remote_copy(
            spectrum.at[pl.ds(f * K, quarter)], west.at[f, pl.ds(0, quarter)],
            halo_send.at[0, f], halo_recv.at[0, f], device_id={"tile": right})
        yield pltpu.make_async_remote_copy(
            spectrum.at[pl.ds(f * K + 3 * quarter, quarter)], west.at[f, pl.ds(quarter, quarter)],
            halo_send.at[1, f], halo_recv.at[1, f], device_id={"tile": right})
        yield pltpu.make_async_remote_copy(
            spectrum.at[pl.ds(f * K + quarter, 2 * quarter)], east.at[f],
            halo_send.at[2, f], halo_recv.at[2, f], device_id={"tile": left})

    masks = [mask_copy(0, right, 0, 0), mask_copy(0, right, 1, 0), mask_copy(1, left, 0, 0), mask_copy(1, left, 1, 0)]
    for copy in masks:
        copy.start()
    for f in range(freqs):
        for copy in halo_copies(f):
            copy.start()

    def find_speed(where, cells, depth):
        def one(t, carry):
            lanes = pl.ds(pl.multiple_of(t * LANES, LANES), LANES)
            wet = cells[:, lanes].astype(F32)
            row = depth[:, lanes]
            sea[where, :, lanes] = wet
            hits = [row == d for d in range(1, DEPTHS)]
            for f in range(freqs):
                j = me * freqs + f
                value = jnp.full((columns, LANES), table[0, j], F32)
                for d in range(1, DEPTHS):
                    value = jnp.where(hits[d - 1], table[d, j], value)
                speed[where, f, :, lanes] = value * wet
            return carry

        lax.fori_loop(0, lane_tiles, one, 0)

    find_speed(0, sea_in, depth_in)
    for copy in masks:
        copy.wait()
    find_speed(1, near_sea.at[0], near_depth.at[0])
    find_speed(2, near_sea.at[1], near_depth.at[1])

    lane = lax.broadcasted_iota(jnp.int32, (columns, rows), 1)
    sub = lax.broadcasted_iota(jnp.int32, (columns, rows), 0)

    def out_copy(f, d):
        target = lax.rem(me + d, parts)
        return pltpu.make_async_remote_copy(
            sent.at[target, 0, :, pl.ds(per * f, per)],
            points.at[0, :, pl.ds(groups * me + per * f, per)],
            out_send.at[0], out_recv.at[0], device_id={"comp": target})

    def out_copy_rest(d):
        target = lax.rem(me + d, parts)
        return pltpu.make_async_remote_copy(
            sent.at[target, 1], points.at[1, :, pl.ds(groups * me, groups)],
            out_send.at[1], out_recv.at[1], device_id={"comp": target})

    def propagate(f, carry):
        chunk_load(f).wait()
        for copy in halo_copies(f):
            copy.wait()
        for quarter in range(4):
            to_east = quarter in (0, 3)
            to_north = quarter in (0, 1)
            halo = west if to_east else east
            place = 1 if to_east else 2
            first = {0: 0, 3: K // 4, 1: 0, 2: K // 4}[quarter]
            x_shift = 1 if to_east else columns - 1
            y_shift = 1 if to_north else rows - 1
            edge = (sub == 0) if to_east else (sub == columns - 1)
            inside = (lane > 0) if to_north else (lane < rows - 1)

            def one(i, carry, quarter=quarter, halo=halo, place=place, first=first, x_shift=x_shift,
                    y_shift=y_shift, edge=edge, inside=inside):
                k = quarter * (K // 4) + i
                along_x, along_y = tab[0, k], tab[1, k]

                def factors(where):
                    cx = speed[where, f] * along_x
                    cy = speed[where, f] * along_y
                    return cx, jnp.where(inside, cy, 0.0), sea[where] - cx - cy

                mine = block[f * K + k].astype(F32)
                theirs = halo[f, first + i].astype(F32)
                cx, cy, keep = factors(0)
                hx, hy, hkeep = factors(place)
                for step in range(PSTEPS):
                    from_halo = pltpu.roll(theirs, x_shift, 0)
                    up_x = jnp.where(edge, from_halo, pltpu.roll(mine, x_shift, 0))
                    mine = keep * mine + cx * up_x + cy * pltpu.roll(mine, y_shift, 1)
                    if step < PSTEPS - 1:
                        theirs = hkeep * theirs + hx * from_halo + hy * pltpu.roll(theirs, y_shift, 1)
                for p in range(lane_tiles):
                    natural[p, pl.ds(pl.multiple_of(k * 8, 8), 8), :] = mine[:, p * LANES:(p + 1) * LANES]
                return carry

            lax.fori_loop(0, K // 4, one, 0)

        def turn(p, carry):
            for c in range(columns):
                for g in range(per):
                    value = natural[p, pl.ds(64 * g + c, 8, stride=8), :]
                    sent[p, c // GCOLS, c % GCOLS, per * f + g] = value.astype(BF16)
            return carry

        lax.fori_loop(0, lane_tiles, turn, 0)
        for d in far_first:
            out_copy(f, d).start()
        return carry

    lax.fori_loop(0, freqs, propagate, 0)
    for d in far_first:
        out_copy_rest(d).start()

    def own_out(g):
        return pltpu.make_async_copy(
            sent.at[me, g], points.at[g, :, pl.ds(groups * me, groups)], own_sem.at[g])

    for g in range(GROUPS):
        own_out(g).start()

    rows_here = pl.ds(pl.multiple_of(me * LANES, LANES), LANES)
    direction = lax.broadcasted_iota(jnp.int32, (K, LANES), 0).astype(F32) * (2.0 * math.pi / K)
    for c in range(columns):
        blow = wind_speed[c:c + 1, rows_here]
        heading = wind_dir[c:c + 1, rows_here]
        align = jnp.maximum(jnp.cos(direction - heading), 0.0)
        winds[c // GCOLS, :, (c % GCOLS) * LANES:(c % GCOLS + 1) * LANES] = blow * align
    couple_load().wait()

    total_comps = parts * comps
    two = 2 * K
    width = GCOLS * LANES

    def own_back(g):
        return pltpu.make_async_copy(
            rounded.at[g, pl.ds(pl.multiple_of(comps * me, comps), comps)], back.at[me, g], own_sem.at[2 + g])

    def source(g, carry):
        pltpu.make_async_copy(
            points.at[g, :, pl.ds(0, groups * (parts - 1))],
            points.at[g, :, pl.ds(0, groups * (parts - 1))], out_recv.at[g]).wait()
        own_out(g).wait()

        def weigh(jj, acc, news):
            for h in range(2):
                folded = news[h][0:8] + news[h][8:16] + news[h][16:24]
                acc = acc + tab[2, 2 * jj + h] * folded
            return acc

        def start(jj, acc):
            at = pl.ds(pl.multiple_of(two * jj, two), two)
            news = []
            for c in range(GCOLS):
                news.append(points[g, c, pl.ds(two // 8 * jj, two // 8)].astype(F32).reshape(two, LANES))
            whole = jnp.concatenate(news, axis=1)
            state[at, :] = whole
            rounded[g, at, :] = whole.astype(BF16)
            return weigh(jj, acc, (whole[:K], whole[K:]))

        zero = jnp.zeros((8, width), F32)
        acc = lax.fori_loop(0, total_comps // two, start, zero)

        def step(s, acc):
            total = jnp.sum(acc, axis=0, keepdims=True)
            sat = jnp.broadcast_to(total / (total + 100.0), (8, width))
            nonlin[...] = jnp.dot(couple[...], rounded[g], preferred_element_type=F32)

            def update(jj, acc):
                news = []
                for h in range(2):
                    at = pl.ds(pl.multiple_of(two * jj + K * h, K), K)
                    j = 2 * jj + h
                    level = 1.0 - tab[4, j] * sat
                    levels = jnp.concatenate([level] * per, axis=0)
                    rate = levels + tab[3, j] * winds[g]
                    new = jnp.maximum(state[at, :] * rate + 0.125 * nonlin[at, :], 0.0)
                    state[at, :] = new
                    news.append(new)
                rounded[g, pl.ds(pl.multiple_of(two * jj, two), two), :] = jnp.concatenate(news, axis=0).astype(BF16)
                return weigh(jj, acc, news)

            return lax.fori_loop(0, total_comps // two, update, zero)

        lax.fori_loop(0, SRC_STEPS, step, acc)
        for d in far_first:
            target = lax.rem(me + d, parts)
            pltpu.make_async_remote_copy(
                rounded.at[g, pl.ds(pl.multiple_of(comps * target, comps), comps)], back.at[me, g],
                back_send.at[g], back_recv.at[g], device_id={"comp": target}).start()
        own_back(g).start()
        return carry

    lax.fori_loop(0, GROUPS, source, 0)

    def settle(g):
        pltpu.make_async_copy(
            back.at[pl.ds(0, parts - 1), g], back.at[pl.ds(0, parts - 1), g], back_recv.at[g]).wait()
        own_back(g).wait()

    settle(0)

    def place(g):
        def one(p, carry):
            for c in range(GCOLS):
                value = back[p, g, :, c * LANES:(c + 1) * LANES].astype(F32)
                turned[p, pl.ds(g * GCOLS + c, comps, stride=8), :] = value
            return carry

        lax.fori_loop(0, lane_tiles, one, 0)

    place(0)
    settle(1)
    place(1)

    def finish(p, carry):
        lanes = pl.ds(pl.multiple_of(p * LANES, LANES), LANES)
        out[:, :, lanes] = turned[p].reshape(comps, columns, LANES).astype(BF16)
        return carry

    lax.fori_loop(0, lane_tiles, finish, 0)

    for g in range(GROUPS):
        pltpu.make_async_copy(
            sent.at[pl.ds(0, parts - 1), g], sent.at[pl.ds(0, parts - 1), g], out_send.at[g]).wait()
        span = pl.ds(0, comps * (parts - 1))
        pltpu.make_async_copy(rounded.at[g, span], rounded.at[g, span], back_send.at[g]).wait()


def on_device(parts, tiles, spectrum, sea_mask, depth_class, group_speed, wind_speed, wind_dir, coupling):
    comps, columns, rows = spectrum.shape
    freqs = comps // K
    whole = comps * parts
    width = GCOLS * LANES
    tab = jnp.asarray(tables())
    vmem, smem, anywhere = (pl.BlockSpec(memory_space=m) for m in (pltpu.VMEM, pltpu.SMEM, pl.ANY))
    dma = pltpu.SemaphoreType.DMA
    return pl.pallas_call(
        functools.partial(step_kernel, parts, tiles),
        out_shape=jax.ShapeDtypeStruct(spectrum.shape, BF16),
        in_specs=[smem, smem, vmem, vmem, vmem, vmem, anywhere, anywhere],
        out_specs=vmem,
        scratch_shapes=[
            pltpu.VMEM((comps, columns, rows), BF16),
            pltpu.VMEM((freqs, K // 2, columns, rows), BF16),
            pltpu.VMEM((freqs, K // 2, columns, rows), BF16),
            pltpu.VMEM((2, columns, rows), jnp.int32),
            pltpu.VMEM((2, columns, rows), jnp.int32),
            pltpu.VMEM((3, freqs, columns, rows), F32),
            pltpu.VMEM((3, columns, rows), F32),
            pltpu.VMEM((parts, K * 8, LANES), F32),
            pltpu.VMEM((parts, GROUPS, GCOLS, comps // 8, 8, LANES), BF16),
            pltpu.VMEM((GROUPS, GCOLS, whole // 8, 8, LANES), BF16),
            pltpu.VMEM((whole, whole), BF16),
            pltpu.VMEM((whole, width), F32),
            pltpu.VMEM((whole, width), F32),
            pltpu.VMEM((GROUPS, whole, width), BF16),
            pltpu.VMEM((GROUPS, K, width), F32),
            pltpu.VMEM((parts, GROUPS, comps, width), BF16),
            pltpu.VMEM((parts, comps * 8, LANES), F32),
            dma((freqs,)), dma,
            dma((2, 2)), dma((2, 2)), dma((3, freqs)), dma((3, freqs)),
            dma((GROUPS,)), dma((GROUPS,)), dma((GROUPS,)), dma((GROUPS,)), dma((2 * GROUPS,)),
        ],
        compiler_params=pltpu.CompilerParams(collective_id=0, has_side_effects=True, vmem_limit_bytes=48 << 20),
    )(tab, group_speed, sea_mask, depth_class, wind_speed, wind_dir, spectrum, coupling)


def solution(mesh):
    placed = (
        P("comp", "tile", None),
        P("tile", None),
        P("tile", None),
        P(),
        P("tile", None),
        P("tile", None),
        P(),
    )
    return jax.shard_map(
        functools.partial(on_device, mesh.shape["comp"], mesh.shape["tile"]),
        mesh=mesh, in_specs=placed, out_specs=P("comp", "tile", None), check_vma=False,
    )
```

profile of v0, /device:TPU:32, one launch (start us, length us, event | category | flops | bytes accessed | tf_op | source)
XLA Modules:
  0.0 109.8 jit_solution(10162190322856066132)
XLA Ops:
  0.0 0.0 copy-start
  0.0 1.4 %copy-done = bf16[96,8,1024]{2,1,0:T(8,128)(2,1)S(1)} copy-done((bf16[96,8,1024]{2,1,0:T(8,128)(2,1)S(1)}, bf16[96,8,1024]{2,1,0:T(8,128)(2,1)}, u32[]{:S(2)}) %copy-start) | copy-done | bytes 1572888
  1.4 0.0 copy-start.1
  1.4 1.3 %copy-done.1 = bf16[768,768]{1,0:T(8,128)(2,1)S(1)} copy-done((bf16[768,768]{1,0:T(8,128)(2,1)S(1)}, bf16[768,768]{1,0:T(8,128)(2,1)}, u32[]{:S(2)}) %copy-start.1) | copy-done | bytes 1179672
  2.7 0.0 copy-start.2
  2.7 0.8 copy-done.2
  3.4 0.0 copy-start.3
  3.4 0.8 copy-done.3
  4.2 0.0 copy-start.4
  4.2 0.8 copy-done.4
  5.0 0.0 copy-start.5
  5.0 0.8 copy-done.5
  5.7 0.0 copy-start.6
  5.7 0.7 copy-done.6
  6.4 0.0 copy-start.7
  6.4 0.7 copy-done.7
  7.1 101.5 %shard_map.82 = bf16[96,8,1024]{2,1,0:T(8,128)(2,1)S(1)} custom-call(f32[5,32]{1,0:T(8,128)S(1)} %copy-done.7, f32[16,32]{1,0:T(8,128)S(1)} %copy-done.6, s32[8,1024]{1,0:T(8,128)S(1)} %copy-done.2, s32[8,1024]{1,0:T(8,128)S(1)} %copy-done.3, f32[8,1024]{1,0:T(8,128)S(1)} %copy-done.4, f32[8,1024]{1,0:T(8,128)S(1)} %copy-done.5, ...), custom_call_target="tpu_custom_call" | custom-call | tf_op jit(solution)/shard_map/pallas_call | solution.py:320
  108.6 1.1 %copy.10 = bf16[96,8,1024]{2,1,0:T(8,128)(2,1)} copy(bf16[96,8,1024]{2,1,0:T(8,128)(2,1)S(1)} %shard_map.82) | data formatting | bytes 3145728
Async XLA Ops:
  0.0 1.4 %copy-start = (bf16[96,8,1024]{2,1,0:T(8,128)(2,1)S(1)}, bf16[96,8,1024]{2,1,0:T(8,128)(2,1)}, u32[]{:S(2)}) copy-start(bf16[96,8,1024]{2,1,0:T(8,128)(2,1)} %spectrum.1) | copy-start | bytes 4718596
  1.4 1.3 %copy-start.1 = (bf16[768,768]{1,0:T(8,128)(2,1)S(1)}, bf16[768,768]{1,0:T(8,128)(2,1)}, u32[]{:S(2)}) copy-start(bf16[768,768]{1,0:T(8,128)(2,1)} %coupling_in.1) | copy-start | bytes 3538948
  2.7 0.8 copy-start.2
  3.4 0.8 copy-start.3
  4.2 0.8 copy-start.4
  5.0 0.8 copy-start.5
  5.7 0.7 copy-start.6
  6.4 0.7 copy-start.7
where the time goes:
time: 111 us; the launch traced here: 110 us
  Pallas kernels  102 us (92%)
  local copies, waits for them, and re-layouts  8.23 us (7%)
    pallas_call x1, Pallas kernels, on_device(): pl.pallas_call(functools.partial(step_kernel, parts, tiles), out_shape=ja...  102 us
    unnamed x17, local copies, waits for them, and re-layouts  8.23 us

commit v1 on v0

--- a/solution.py
+++ b/solution.py
@@ -36,10 +36,10 @@
 
 def step_kernel(
     parts, tiles,
-    tab, table, sea_in, depth_in, wind_speed, wind_dir, spectrum, coupling_in, out,
-    block, west, east, near_sea, near_depth, speed, sea, natural, sent, points, couple,
+    tab_in, table_in, sea_in, depth_in, speed_in, dir_in, spectrum, coupling_in, out,
+    tab, table, sea_own, depth_own, wind_speed, wind_dir, block, west, east, near_sea, near_depth, speed, sea, natural, sent, points, couple,
     state, nonlin, rounded, winds, back, turned,
-    load_sem, couple_sem, mask_send, mask_recv, halo_send, halo_recv,
+    small_sem, load_sem, couple_sem, mask_send, mask_recv, halo_send, halo_recv,
     out_send, out_recv, back_send, back_recv, own_sem,
 ):
     me = lax.axis_index("comp")
@@ -60,8 +60,18 @@
     def couple_load():
         return pltpu.make_async_copy(coupling_in, couple, couple_sem)
 
+    smalls = [
+        pltpu.make_async_copy(source, target, small_sem.at[i])
+        for i, (source, target) in enumerate((
+            (table_in, table), (sea_in, sea_own), (depth_in, depth_own),
+            (tab_in, tab), (speed_in, wind_speed), (dir_in, wind_dir)))
+    ]
+    for copy in smalls[:4]:
+        copy.start()
     for f in range(freqs):
         chunk_load(f).start()
+    for copy in smalls[4:]:
+        copy.start()
     couple_load().start()
 
     barrier = pltpu.get_barrier_semaphore()
@@ -69,6 +79,8 @@
         pl.semaphore_signal(barrier, 1, device_id={"comp": lax.rem(me + d, parts)})
     for side in (left, right):
         pl.semaphore_signal(barrier, 1, device_id={"tile": side})
+    for copy in smalls[:4]:
+        copy.wait()
     pl.semaphore_wait(barrier, parts + 1)
 
     def mask_copy(side, target, array, which):
@@ -87,9 +99,11 @@
         yield pltpu.make_async_remote_copy(
             spectrum.at[pl.ds(f * K + 3 * quarter, quarter)], west.at[f, pl.ds(quarter, quarter)],
             halo_send.at[1, f], halo_recv.at[1, f], device_id={"tile": right})
-        yield pltpu.make_async_remote_copy(
-            spectrum.at[pl.ds(f * K + quarter, 2 * quarter)], east.at[f],
-            halo_send.at[2, f], halo_recv.at[2, f], device_id={"tile": left})
+        for half in range(2):
+            yield pltpu.make_async_remote_copy(
+                spectrum.at[pl.ds(f * K + (1 + half) * quarter, quarter)],
+                east.at[f, pl.ds(half * quarter, quarter)],
+                halo_send.at[2 + half, f], halo_recv.at[2 + half, f], device_id={"tile": left})
 
     masks = [mask_copy(0, right, 0, 0), mask_copy(0, right, 1, 0), mask_copy(1, left, 0, 0), mask_copy(1, left, 1, 0)]
     for copy in masks:
@@ -115,7 +129,7 @@
 
         lax.fori_loop(0, lane_tiles, one, 0)
 
-    find_speed(0, sea_in, depth_in)
+    find_speed(0, sea_own, depth_own)
     for copy in masks:
         copy.wait()
     find_speed(1, near_sea.at[0], near_depth.at[0])
@@ -139,9 +153,9 @@
 
     def propagate(f, carry):
         chunk_load(f).wait()
-        for copy in halo_copies(f):
-            copy.wait()
+        halos = list(halo_copies(f))
         for quarter in range(4):
+            halos[(0, 2, 3, 1)[quarter]].wait()
             to_east = quarter in (0, 3)
             to_north = quarter in (0, 1)
             halo = west if to_east else east
@@ -176,7 +190,7 @@
                     natural[p, pl.ds(pl.multiple_of(k * 8, 8), 8), :] = mine[:, p * LANES:(p + 1) * LANES]
                 return carry
 
-            lax.fori_loop(0, K // 4, one, 0)
+            lax.fori_loop(0, K // 4, one, 0, unroll=3)
 
         def turn(p, carry):
             for c in range(columns):
@@ -203,6 +217,8 @@
 
     rows_here = pl.ds(pl.multiple_of(me * LANES, LANES), LANES)
     direction = lax.broadcasted_iota(jnp.int32, (K, LANES), 0).astype(F32) * (2.0 * math.pi / K)
+    for copy in smalls[4:]:
+        copy.wait()
     for c in range(columns):
         blow = wind_speed[c:c + 1, rows_here]
         heading = wind_dir[c:c + 1, rows_here]
@@ -315,14 +331,20 @@
     whole = comps * parts
     width = GCOLS * LANES
     tab = jnp.asarray(tables())
-    vmem, smem, anywhere = (pl.BlockSpec(memory_space=m) for m in (pltpu.VMEM, pltpu.SMEM, pl.ANY))
+    hbm = pl.BlockSpec(memory_space=pltpu.HBM)
     dma = pltpu.SemaphoreType.DMA
     return pl.pallas_call(
         functools.partial(step_kernel, parts, tiles),
         out_shape=jax.ShapeDtypeStruct(spectrum.shape, BF16),
-        in_specs=[smem, smem, vmem, vmem, vmem, vmem, anywhere, anywhere],
-        out_specs=vmem,
+        in_specs=[hbm] * 8,
+        out_specs=pl.BlockSpec(memory_space=pltpu.VMEM),
         scratch_shapes=[
+            pltpu.SMEM(tab.shape, F32),
+            pltpu.SMEM(group_speed.shape, F32),
+            pltpu.VMEM((columns, rows), jnp.int32),
+            pltpu.VMEM((columns, rows), jnp.int32),
+            pltpu.VMEM((columns, rows), F32),
+            pltpu.VMEM((columns, rows), F32),
             pltpu.VMEM((comps, columns, rows), BF16),
             pltpu.VMEM((freqs, K // 2, columns, rows), BF16),
             pltpu.VMEM((freqs, K // 2, columns, rows), BF16),
@@ -340,12 +362,12 @@
             pltpu.VMEM((GROUPS, K, width), F32),
             pltpu.VMEM((parts, GROUPS, comps, width), BF16),
             pltpu.VMEM((parts, comps * 8, LANES), F32),
-            dma((freqs,)), dma,
-            dma((2, 2)), dma((2, 2)), dma((3, freqs)), dma((3, freqs)),
+            dma((6,)), dma((freqs,)), dma,
+            dma((2, 2)), dma((2, 2)), dma((4, freqs)), dma((4, freqs)),
             dma((GROUPS,)), dma((GROUPS,)), dma((GROUPS,)), dma((GROUPS,)), dma((2 * GROUPS,)),
         ],
         compiler_params=pltpu.CompilerParams(collective_id=0, has_side_effects=True, vmem_limit_bytes=48 << 20),
-    )(tab, group_speed, sea_mask, depth_class, wind_speed, wind_dir, spectrum, coupling)
+    )(*(pltpu.with_memory_space_constraint(a, pltpu.HBM) for a in (tab, group_speed, sea_mask, depth_class, wind_speed, wind_dir, spectrum, coupling)))
 
 
 def solution(mesh):

time: 111 us -> 87.6 us (0.79)
  Pallas kernels: 102 us -> 85.4 us
  local copies, waits for them, and re-layouts: 8.23 us -> 1.15 us
    pallas_call x1, Pallas kernels: 102 us -> 85.4 us  [on_device(): pl.pallas_call(functools.partial(step_kernel, parts, tiles), out_shape=ja...]
    unnamed x17 -> x1, local copies, waits for them, and re-layouts: 8.23 us -> 1.15 us
where the time goes in v1:
time: 87.6 us; the launch traced here: 86.5 us
  Pallas kernels  85.4 us (97%)
  local copies, waits for them, and re-layouts  1.15 us (1%)
    pallas_call x1, Pallas kernels, on_device(): pl.pallas_call(functools.partial(step_kernel, parts, tiles), out_shape=ja...  85.4 us

profile of v1, /device:TPU:32, one launch (start us, length us, event | category | flops | bytes accessed | tf_op | source)
XLA Modules:
  0.0 86.5 jit_solution(15793859922712912901)
XLA Ops:
  0.0 85.4 %shard_map.82 = bf16[96,8,1024]{2,1,0:T(8,128)(2,1)S(1)} custom-call(f32[5,32]{1,0:T(8,128)} %constant.2.clone.tab_in, f32[16,32]{1,0:T(8,128)} %table_in.1, s32[8,1024]{1,0:T(8,128)} %sea_in.1, s32[8,1024]{1,0:T(8,128)} %depth_in.1, f32[8,1024]{1,0:T(8,128)} %speed_in.1, f32[8,1024]{1,0:T(8,128)} %dir_in.1, bf16[96,8,1024]{2,1,0:T(8,128)(2,1)} %spectrum.1, ...), custom_call_target="tpu_custom_call" | custom-call | tf_op jit(solution)/shard_map/pallas_call | solution.py:336
  85.4 1.1 %copy.10 = bf16[96,8,1024]{2,1,0:T(8,128)(2,1)} copy(bf16[96,8,1024]{2,1,0:T(8,128)(2,1)S(1)} %shard_map.82) | data formatting | bytes 3145728

commit v2 on v1

v2 whole, which is shorter than its diff:
```python
import functools
import math

import jax
import jax.numpy as jnp
import numpy as np
from jax import lax
from jax.experimental import pallas as pl
from jax.experimental.pallas import tpu as pltpu
from jax.sharding import PartitionSpec as P

K = 24
F = 32
DEPTHS = 16
PSTEPS = 4
SRC_STEPS = 4
COLS = 8
LANES = 128
GROUPS = 2
GCOLS = COLS // GROUPS
BF16 = jnp.bfloat16
F32 = jnp.float32


def tables():
    theta = np.arange(K).astype(np.float32) * np.float32(2.0 * math.pi / K)
    j = np.arange(F).astype(np.float64)
    rows = np.zeros((5, F), np.float32)
    rows[0, :K] = np.abs(np.cos(theta))
    rows[1, :K] = np.abs(np.sin(theta))
    rows[2] = 0.1 * 1.1**j
    rows[3] = 0.5 * 0.004 * 1.1 ** (j - 16.0)
    rows[4] = 0.5 * 0.3 * (j + 1.0) / F
    return rows


def step_kernel(
    parts, tiles,
    tab_in, table_in, sea_in, depth_in, speed_in, dir_in, spectrum, coupling_in, out,
    tab, table, sea_own, depth_own, wind_speed, wind_dir, block, west, east, near_sea, near_depth, speed, sea, natural, sent, points, couple,
    state, nonlin, rounded, winds, back, turned,
    small_sem, load_sem, couple_sem, mask_send, mask_recv, halo_send, halo_recv,
    out_send, out_recv, back_send, back_recv, own_sem,
):
    me = lax.axis_index("comp")
    tile = lax.axis_index("tile")
    left = lax.rem(tile + tiles - 1, tiles)
    right = lax.rem(tile + 1, tiles)
    comps, columns, rows = block.shape
    freqs = comps // K
    lane_tiles = rows // LANES
    groups = comps // 8
    per = K // 8
    near_first = sorted(range(1, parts), key=lambda d: min(d, parts - d))

    def chunk_load(f):
        part = pl.ds(f * K, K)
        return pltpu.make_async_copy(spectrum.at[part], block.at[part], load_sem.at[f])

    def couple_load():
        return pltpu.make_async_copy(coupling_in, couple, couple_sem)

    smalls = [
        pltpu.make_async_copy(source, target, small_sem.at[i])
        for i, (source, target) in enumerate((
            (table_in, table), (sea_in, sea_own), (depth_in, depth_own),
            (tab_in, tab), (speed_in, wind_speed), (dir_in, wind_dir)))
    ]
    for copy in smalls[:4]:
        copy.start()
    for f in range(freqs):
        chunk_load(f).start()
    for copy in smalls[4:]:
        copy.start()
    couple_load().start()

    barrier = pltpu.get_barrier_semaphore()
    for d in range(1, parts):
        pl.semaphore_signal(barrier, 1, device_id={"comp": lax.rem(me + d, parts)})
    for side in (left, right):
        pl.semaphore_signal(barrier, 1, device_id={"tile": side})

    quarter_of = K // 4
    half = columns // 2
    lane = lax.broadcasted_iota(jnp.int32, (columns, rows), 1)
    sub = lax.broadcasted_iota(jnp.int32, (columns, rows), 0)
    sub_one = lax.broadcasted_iota(jnp.int32, (columns, LANES), 0)

    def find_speed(window, low_sea, high_sea, low_depth, high_depth):
        def one(t, carry):
            lanes = pl.ds(pl.multiple_of(t * LANES, LANES), LANES)
            wet, row = low_sea[:, lanes].astype(F32), low_depth[:, lanes].astype(F32)
            if window:
                wet = jnp.where(sub_one < half, wet, high_sea[:, lanes].astype(F32))
                row = jnp.where(sub_one < half, row, high_depth[:, lanes].astype(F32))
            sea[window, :, lanes] = wet
            hits = [row == d for d in range(1, DEPTHS)]
            for f in range(freqs):
                j = me * freqs + f
                value = jnp.full((columns, LANES), table[0, j], F32)
                for d in range(1, DEPTHS):
                    value = jnp.where(hits[d - 1], table[d, j], value)
                speed[window, f, :, lanes] = value * wet
            return carry

        lax.fori_loop(0, lane_tiles, one, 0)

    def run(alone, beside, f, quarter, low, count, unroll):
        to_east = quarter in (0, 3)
        to_north = quarter in (0, 1)
        halo = west if to_east else east
        first = quarter_of if quarter in (2, 3) else 0
        x_shift = 1 if to_east else columns - 1
        y_shift = 1 if to_north else rows - 1
        inside = (lane > 0) if to_north else (lane < rows - 1)
        windows = ([0] if alone else []) + ([1 if to_east else 2] if beside else [])

        def one(i, carry):
            k = quarter * quarter_of + low + i
            mine = block[f * K + k].astype(F32)
            results = []
            for window in windows:
                energy = mine
                if window:
                    theirs = halo[f, first + low + i].astype(F32)
                    pair = (mine, theirs) if to_east else (theirs, mine)
                    energy = jnp.where(sub < half, *pair)
                cx = speed[window, f] * tab[0, k]
                cy = speed[window, f] * tab[1, k]
                keep = sea[window] - cx - cy
                cy = jnp.where(inside, cy, 0.0)
                for step in range(PSTEPS):
                    energy = keep * energy + cx * pltpu.roll(energy, x_shift, 0) + cy * pltpu.roll(energy, y_shift, 1)
                results.append(energy)
            at = pl.ds(pl.multiple_of(k * 8, 8), 8)
            for p in range(lane_tiles):
                pieces = [energy[:, p * LANES:(p + 1) * LANES] for energy in results]
                if beside:
                    other = pieces[0] if alone else natural[f, p, at, :]
                    pair = (pieces[-1], other) if to_east else (other, pieces[-1])
                    pieces = [jnp.where(sub_one < half, *pair)]
                natural[f, p, at, :] = pieces[0]
            return carry

        lax.fori_loop(0, count, one, 0, unroll=unroll)

    def slot(f, g):
        return f if g == 1 else freqs + 2 * f + g // 2

    def turn(f, pieces):
        def one(p, carry):
            for c, g in pieces:
                value = natural[f, p, pl.ds(64 * g + c, 8, stride=8), :]
                sent[p, c // GCOLS, c % GCOLS, slot(f, g)] = value.astype(BF16)
            return carry

        lax.fori_loop(0, lane_tiles, one, 0)

    early = [(c, 1) for c in range(GCOLS)]
    late = [(c, g) for c in range(columns) for g in range(per) if (c, g) not in early]

    def out_copy(g, low, count, d):
        target = lax.rem(me + d, parts)
        return pltpu.make_async_remote_copy(
            sent.at[target, g, :, pl.ds(low, count)], points.at[g, :, pl.ds(groups * me + low, count)],
            out_send.at[g], out_recv.at[g], device_id={"comp": target})

    for copy in smalls[:4]:
        copy.wait()
    find_speed(0, sea_own, None, depth_own, None)

    def start_alone(f, carry):
        chunk_load(f).wait()
        run(True, False, f, 1, 2, 4, 4)
        run(True, False, f, 2, 0, 4, 4)
        turn(f, early)
        return carry

    lax.fori_loop(0, freqs, start_alone, 0)
    pl.semaphore_wait(barrier, parts + 1)

    def mask_copy(side, target, array):
        return pltpu.make_async_remote_copy(
            (sea_in, depth_in)[array],
            (near_sea, near_depth)[array].at[side],
            mask_send.at[side, array], mask_recv.at[side, array],
            device_id={"tile": target},
        )

    def halo_copies(f):
        for part, (first, array, low, target) in enumerate((
                (0, west, 0, right), (1, east, 0, left), (2, east, 1, left), (3, west, 1, right))):
            yield pltpu.make_async_remote_copy(
                spectrum.at[pl.ds(f * K + first * quarter_of, quarter_of)],
                array.at[f, pl.ds(low * quarter_of, quarter_of)],
                halo_send.at[part, f], halo_recv.at[part, f], device_id={"tile": target})

    masks = [mask_copy(side, target, array) for side, target in ((0, right), (1, left)) for array in range(2)]
    for copy in masks:
        copy.start()
    for f in range(freqs):
        for copy in halo_copies(f):
            copy.start()
    for d in near_first:
        out_copy(0, 0, freqs, d).start()

    for copy in masks:
        copy.wait()
    find_speed(1, sea_own, near_sea.at[0], depth_own, near_depth.at[0])
    find_speed(2, near_sea.at[1], sea_own, near_depth.at[1], depth_own)

    def with_halo(f, carry):
        halos = list(halo_copies(f))
        halos[0].wait()
        run(True, True, f, 0, 0, 6, 3)
        halos[1].wait()
        run(True, True, f, 1, 0, 2, 2)
        run(False, True, f, 1, 2, 4, 4)
        halos[2].wait()
        run(False, True, f, 2, 0, 4, 4)
        run(True, True, f, 2, 4, 2, 2)
        halos[3].wait()
        run(True, True, f, 3, 0, 6, 3)
        turn(f, late)
        for d in near_first:
            out_copy(0, freqs + 2 * f, 2, d).start()
        return carry

    lax.fori_loop(0, freqs, with_halo, 0)
    for d in near_first:
        out_copy(1, 0, groups, d).start()

    def own_out(g):
        return pltpu.make_async_copy(
            sent.at[me, g], points.at[g, :, pl.ds(groups * me, groups)], own_sem.at[g])

    for g in range(GROUPS):
        own_out(g).start()

    rows_here = pl.ds(pl.multiple_of(me * LANES, LANES), LANES)
    direction = lax.broadcasted_iota(jnp.int32, (K, LANES), 0).astype(F32) * (2.0 * math.pi / K)
    for copy in smalls[4:]:
        copy.wait()
    for c in range(columns):
        blow = wind_speed[c:c + 1, rows_here]
        heading = wind_dir[c:c + 1, rows_here]
        align = jnp.maximum(jnp.cos(direction - heading), 0.0)
        winds[c // GCOLS, :, (c % GCOLS) * LANES:(c % GCOLS + 1) * LANES] = blow * align
    couple_load().wait()

    total_comps = parts * comps
    two = 2 * K
    width = GCOLS * LANES

    def own_back(g):
        return pltpu.make_async_copy(
            rounded.at[g, pl.ds(pl.multiple_of(comps * me, comps), comps)], back.at[me, g], own_sem.at[2 + g])

    def source(g, carry):
        pltpu.make_async_copy(
            points.at[g, :, pl.ds(0, groups * (parts - 1))],
            points.at[g, :, pl.ds(0, groups * (parts - 1))], out_recv.at[g]).wait()
        own_out(g).wait()

        def weigh(jj, acc, news):
            for h in range(2):
                folded = news[h][0:8] + news[h][8:16] + news[h][16:24]
                acc = acc + tab[2, 2 * jj + h] * folded
            return acc

        def start(z, acc):
            for pair in range(freqs // 2):
                at = pl.ds(pl.multiple_of(comps * z + two * pair, two), two)
                lanes = []
                for c in range(GCOLS):
                    lanes.append(jnp.concatenate([
                        points[g, c, groups * z + slot(2 * pair + h, i)].astype(F32)
                        for h in range(2) for i in range(per)], axis=0))
                whole = jnp.concatenate(lanes, axis=1)
                state[at, :] = whole
                rounded[g, at, :] = whole.astype(BF16)
                acc = weigh(freqs // 2 * z + pair, acc, (whole[:K], whole[K:]))
            return acc

        zero = jnp.zeros((8, width), F32)
        acc = lax.fori_loop(0, parts, start, zero)

        def step(s, acc):
            total = jnp.sum(acc, axis=0, keepdims=True)
            sat = jnp.broadcast_to(total / (total + 100.0), (8, width))
            nonlin[...] = jnp.dot(couple[...], rounded[g], preferred_element_type=F32)

            def update(jj, acc):
                news = []
                for h in range(2):
                    at = pl.ds(pl.multiple_of(two * jj + K * h, K), K)
                    j = 2 * jj + h
                    level = 1.0 - tab[4, j] * sat
                    levels = jnp.concatenate([level] * per, axis=0)
                    rate = levels + tab[3, j] * winds[g]
                    new = jnp.maximum(state[at, :] * rate + 0.125 * nonlin[at, :], 0.0)
                    state[at, :] = new
                    news.append(new)
                rounded[g, pl.ds(pl.multiple_of(two * jj, two), two), :] = jnp.concatenate(news, axis=0).astype(BF16)
                return weigh(jj, acc, news)

            return lax.fori_loop(0, total_comps // two, update, zero)

        lax.fori_loop(0, SRC_STEPS, step, acc)
        for d in near_first:
            target = lax.rem(me + d, parts)
            pltpu.make_async_remote_copy(
                rounded.at[g, pl.ds(pl.multiple_of(comps * target, comps), comps)], back.at[me, g],
                back_send.at[g], back_recv.at[g, g * d], device_id={"comp": target}).start()
        own_back(g).start()
        return carry

    lax.fori_loop(0, GROUPS, source, 0)

    pltpu.make_async_copy(
        back.at[pl.ds(0, parts - 1), 0], back.at[pl.ds(0, parts - 1), 0], back_recv.at[0, 0]).wait()
    own_back(0).wait()

    def place(p, g):
        for c in range(GCOLS):
            value = back[p, g, :, c * LANES:(c + 1) * LANES].astype(F32)
            turned[p, pl.ds(g * GCOLS + c, comps, stride=8), :] = value

    def place_first(p, carry):
        place(p, 0)
        return carry

    lax.fori_loop(0, lane_tiles, place_first, 0)

    def finish(p):
        place(p, 1)
        lanes = pl.ds(pl.multiple_of(p * LANES, LANES), LANES)
        out[:, :, lanes] = turned[p].reshape(comps, columns, LANES).astype(BF16)

    own_back(1).wait()
    finish(me)

    def arrived(i, carry):
        d = (i % 2) * (parts - 1 - i // 2) + (1 - i % 2) * (1 + i // 2)
        pltpu.make_async_copy(back.at[0, 1], back.at[0, 1], back_recv.at[1, d]).wait()
        finish(lax.rem(me + parts - d, parts))
        return carry

    lax.fori_loop(0, parts - 1, arrived, 0)

    for g in range(GROUPS):
        pltpu.make_async_copy(
            sent.at[pl.ds(0, parts - 1), g], sent.at[pl.ds(0, parts - 1), g], out_send.at[g]).wait()
        span = pl.ds(0, comps * (parts - 1))
        pltpu.make_async_copy(rounded.at[g, span], rounded.at[g, span], back_send.at[g]).wait()


def on_device(parts, tiles, spectrum, sea_mask, depth_class, group_speed, wind_speed, wind_dir, coupling):
    comps, columns, rows = spectrum.shape
    freqs = comps // K
    whole = comps * parts
    width = GCOLS * LANES
    tab = jnp.asarray(tables())
    hbm = pl.BlockSpec(memory_space=pltpu.HBM)
    dma = pltpu.SemaphoreType.DMA
    return pl.pallas_call(
        functools.partial(step_kernel, parts, tiles),
        out_shape=jax.ShapeDtypeStruct(spectrum.shape, BF16),
        in_specs=[hbm] * 8,
        out_specs=pl.BlockSpec(memory_space=pltpu.VMEM),
        scratch_shapes=[
            pltpu.SMEM(tab.shape, F32),
            pltpu.SMEM(group_speed.shape, F32),
            pltpu.VMEM((columns, rows), jnp.int32),
            pltpu.VMEM((columns, rows), jnp.int32),
            pltpu.VMEM((columns, rows), F32),
            pltpu.VMEM((columns, rows), F32),
            pltpu.VMEM((comps, columns, rows), BF16),
            pltpu.VMEM((freqs, K // 2, columns, rows), BF16),
            pltpu.VMEM((freqs, K // 2, columns, rows), BF16),
            pltpu.VMEM((2, columns, rows), jnp.int32),
            pltpu.VMEM((2, columns, rows), jnp.int32),
            pltpu.VMEM((3, freqs, columns, rows), F32),
            pltpu.VMEM((3, columns, rows), F32),
            pltpu.VMEM((freqs, parts, K * 8, LANES), F32),
            pltpu.VMEM((parts, GROUPS, GCOLS, comps // 8, 8, LANES), BF16),
            pltpu.VMEM((GROUPS, GCOLS, whole // 8, 8, LANES), BF16),
            pltpu.VMEM((whole, whole), BF16),
            pltpu.VMEM((whole, width), F32),
            pltpu.VMEM((whole, width), F32),
            pltpu.VMEM((GROUPS, whole, width), BF16),
            pltpu.VMEM((GROUPS, K, width), F32),
            pltpu.VMEM((parts, GROUPS, comps, width), BF16),
            pltpu.VMEM((parts, comps * 8, LANES), F32),
            dma((6,)), dma((freqs,)), dma,
            dma((2, 2)), dma((2, 2)), dma((4, freqs)), dma((4, freqs)),
            dma((GROUPS,)), dma((GROUPS,)), dma((GROUPS,)), dma((GROUPS, parts)), dma((2 * GROUPS,)),
        ],
        compiler_params=pltpu.CompilerParams(collective_id=0, has_side_effects=True, vmem_limit_bytes=48 << 20),
    )(*(pltpu.with_memory_space_constraint(a, pltpu.HBM) for a in (tab, group_speed, sea_mask, depth_class, wind_speed, wind_dir, spectrum, coupling)))


def solution(mesh):
    placed = (
        P("comp", "tile", None),
        P("tile", None),
        P("tile", None),
        P(),
        P("tile", None),
        P("tile", None),
        P(),
    )
    return jax.shard_map(
        functools.partial(on_device, mesh.shape["comp"], mesh.shape["tile"]),
        mesh=mesh, in_specs=placed, out_specs=P("comp", "tile", None), check_vma=False,
    )
```

time: 87.6 us -> 82.7 us (0.944); the launches traced: 86.5 us -> 82.6 us
  Pallas kernels: 85.4 us -> 81.4 us
    pallas_call x1, Pallas kernels: 85.4 us -> 81.4 us  [on_device(): pl.pallas_call(functools.partial(step_kernel, parts, tiles), out_shape=ja...]
where the time goes in v2:
time: 82.7 us; the launch traced here: 82.6 us
  Pallas kernels  81.4 us (98%)
  local copies, waits for them, and re-layouts  1.15 us (1%)
    pallas_call x1, Pallas kernels, on_device(): pl.pallas_call(functools.partial(step_kernel, parts, tiles), out_shape=ja...  81.4 us

profile of v2, /device:TPU:32, one launch (start us, length us, event | category | flops | bytes accessed | tf_op | source)
XLA Modules:
  0.0 82.6 jit_solution(17437112183262427117)
XLA Ops:
  0.0 81.4 %shard_map.82 = bf16[96,8,1024]{2,1,0:T(8,128)(2,1)S(1)} custom-call(f32[5,32]{1,0:T(8,128)} %constant.2.clone.tab_in, f32[16,32]{1,0:T(8,128)} %table_in.1, s32[8,1024]{1,0:T(8,128)} %sea_in.1, s32[8,1024]{1,0:T(8,128)} %depth_in.1, f32[8,1024]{1,0:T(8,128)} %speed_in.1, f32[8,1024]{1,0:T(8,128)} %dir_in.1, bf16[96,8,1024]{2,1,0:T(8,128)(2,1)} %spectrum.1, ...), custom_call_target="tpu_custom_call" | custom-call | tf_op jit(solution)/shard_map/pallas_call | solution.py:366
  81.4 1.1 %copy.10 = bf16[96,8,1024]{2,1,0:T(8,128)(2,1)} copy(bf16[96,8,1024]{2,1,0:T(8,128)(2,1)S(1)} %shard_map.82) | data formatting | bytes 3145728

commit v3 on v2

--- a/solution.py
+++ b/solution.py
@@ -87,23 +87,21 @@
     sub_one = lax.broadcasted_iota(jnp.int32, (columns, LANES), 0)
 
     def find_speed(window, low_sea, high_sea, low_depth, high_depth):
-        def one(t, carry):
-            lanes = pl.ds(pl.multiple_of(t * LANES, LANES), LANES)
-            wet, row = low_sea[:, lanes].astype(F32), low_depth[:, lanes].astype(F32)
-            if window:
-                wet = jnp.where(sub_one < half, wet, high_sea[:, lanes].astype(F32))
-                row = jnp.where(sub_one < half, row, high_depth[:, lanes].astype(F32))
-            sea[window, :, lanes] = wet
-            hits = [row == d for d in range(1, DEPTHS)]
-            for f in range(freqs):
-                j = me * freqs + f
-                value = jnp.full((columns, LANES), table[0, j], F32)
-                for d in range(1, DEPTHS):
-                    value = jnp.where(hits[d - 1], table[d, j], value)
-                speed[window, f, :, lanes] = value * wet
+        wet, row = low_sea[...].astype(F32), low_depth[...].astype(F32)
+        if window:
+            wet = jnp.where(sub < half, wet, high_sea[...].astype(F32))
+            row = jnp.where(sub < half, row, high_depth[...].astype(F32))
+        sea[window] = wet
+
+        def one(f, carry):
+            j = me * freqs + f
+            value = jnp.full((columns, rows), table[0, j], F32)
+            for d in range(1, DEPTHS):
+                value = jnp.where(row == d, table[d, j], value)
+            speed[window, f] = value * wet
             return carry
 
-        lax.fori_loop(0, lane_tiles, one, 0)
+        lax.fori_loop(0, freqs, one, 0)
 
     def run(alone, beside, f, quarter, low, count, unroll):
         to_east = quarter in (0, 3)
@@ -157,7 +155,7 @@
         lax.fori_loop(0, lane_tiles, one, 0)
 
     early = [(c, 1) for c in range(GCOLS)]
-    late = [(c, g) for c in range(columns) for g in range(per) if (c, g) not in early]
+    late = [(c, g) for c in range(GCOLS, columns) for g in range(per)]
 
     def out_copy(g, low, count, d):
         target = lax.rem(me + d, parts)
@@ -176,7 +174,7 @@
         turn(f, early)
         return carry
 
-    lax.fori_loop(0, freqs, start_alone, 0)
+    start_alone(0, 0)
     pl.semaphore_wait(barrier, parts + 1)
 
     def mask_copy(side, target, array):
@@ -201,13 +199,21 @@
     for f in range(freqs):
         for copy in halo_copies(f):
             copy.start()
-    for d in near_first:
-        out_copy(0, 0, freqs, d).start()
+    for f in range(freqs):
+        if f:
+            start_alone(f, 0)
+        for d in near_first:
+            out_copy(0, f, 1, d).start()
 
     for copy in masks:
         copy.wait()
     find_speed(1, sea_own, near_sea.at[0], depth_own, near_depth.at[0])
     find_speed(2, near_sea.at[1], sea_own, near_depth.at[1], depth_own)
+
+    def finished(f, g):
+        turn(f, [(c, g) for c in range(GCOLS)])
+        for d in near_first:
+            out_copy(0, slot(f, g), 1, d).start()
 
     def with_halo(f, carry):
         halos = list(halo_copies(f))
@@ -215,15 +221,15 @@
         run(True, True, f, 0, 0, 6, 3)
         halos[1].wait()
         run(True, True, f, 1, 0, 2, 2)
+        finished(f, 0)
         run(False, True, f, 1, 2, 4, 4)
         halos[2].wait()
         run(False, True, f, 2, 0, 4, 4)
         run(True, True, f, 2, 4, 2, 2)
         halos[3].wait()
         run(True, True, f, 3, 0, 6, 3)
+        finished(f, 2)
         turn(f, late)
-        for d in near_first:
-            out_copy(0, freqs + 2 * f, 2, d).start()
         return carry
 
     lax.fori_loop(0, freqs, with_halo, 0)

time: 82.7 us -> 80.5 us (0.973)
  Pallas kernels: 81.4 us -> 79.3 us
    pallas_call x1, Pallas kernels: 81.4 us -> 79.3 us  [on_device(): pl.pallas_call(functools.partial(step_kernel, parts, tiles), out_shape=ja...]
where the time goes in v3:
time: 80.5 us; the launch traced here: 80.4 us
  Pallas kernels  79.3 us (99%)
  local copies, waits for them, and re-layouts  1.15 us (1%)
    pallas_call x1, Pallas kernels, on_device(): pl.pallas_call(functools.partial(step_kernel, parts, tiles), out_shape=ja...  79.3 us

profile of v3, /device:TPU:32, one launch (start us, length us, event | category | flops | bytes accessed | tf_op | source)
XLA Modules:
  0.0 80.4 jit_solution(17961039418628807971)
XLA Ops:
  0.0 79.3 %shard_map.82 = bf16[96,8,1024]{2,1,0:T(8,128)(2,1)S(1)} custom-call(f32[5,32]{1,0:T(8,128)} %constant.2.clone.tab_in, f32[16,32]{1,0:T(8,128)} %table_in.1, s32[8,1024]{1,0:T(8,128)} %sea_in.1, s32[8,1024]{1,0:T(8,128)} %depth_in.1, f32[8,1024]{1,0:T(8,128)} %speed_in.1, f32[8,1024]{1,0:T(8,128)} %dir_in.1, bf16[96,8,1024]{2,1,0:T(8,128)(2,1)} %spectrum.1, ...), custom_call_target="tpu_custom_call" | custom-call | tf_op jit(solution)/shard_map/pallas_call | solution.py:372
  79.3 1.1 %copy.10 = bf16[96,8,1024]{2,1,0:T(8,128)(2,1)} copy(bf16[96,8,1024]{2,1,0:T(8,128)(2,1)S(1)} %shard_map.82) | data formatting | bytes 3145728

commit v4 on v3

--- a/solution.py
+++ b/solution.py
@@ -18,6 +18,7 @@
 LANES = 128
 GROUPS = 2
 GCOLS = COLS // GROUPS
+AHEAD = 1
 BF16 = jnp.bfloat16
 F32 = jnp.float32
 
@@ -230,11 +231,21 @@
         run(True, True, f, 3, 0, 6, 3)
         finished(f, 2)
         turn(f, late)
+
+        @pl.when(f < AHEAD)
+        def _():
+            for d in near_first:
+                out_copy(1, f, 1, d).start()
+            for d in near_first:
+                out_copy(1, freqs + 2 * f, 2, d).start()
+
         return carry
 
     lax.fori_loop(0, freqs, with_halo, 0)
     for d in near_first:
-        out_copy(1, 0, groups, d).start()
+        out_copy(1, AHEAD, freqs - AHEAD, d).start()
+    for d in near_first:
+        out_copy(1, freqs + 2 * AHEAD, 2 * (freqs - AHEAD), d).start()
 
     def own_out(g):
         return pltpu.make_async_copy(

time: 80.5 us -> 79.8 us (level)
  no operation moved by 1% of the time
where the time goes in v4:
time: 79.8 us; the launch traced here: 79.7 us
  Pallas kernels  78.5 us (98%)
  local copies, waits for them, and re-layouts  1.15 us (1%)
    pallas_call x1, Pallas kernels, on_device(): pl.pallas_call(functools.partial(step_kernel, parts, tiles), out_shape=ja...  78.5 us

profile of v4, /device:TPU:32, one launch (start us, length us, event | category | flops | bytes accessed | tf_op | source)
XLA Modules:
  0.0 79.7 jit_solution(9406713269353281043)
XLA Ops:
  0.0 78.5 %shard_map.82 = bf16[96,8,1024]{2,1,0:T(8,128)(2,1)S(1)} custom-call(f32[5,32]{1,0:T(8,128)} %constant.2.clone.tab_in, f32[16,32]{1,0:T(8,128)} %table_in.1, s32[8,1024]{1,0:T(8,128)} %sea_in.1, s32[8,1024]{1,0:T(8,128)} %depth_in.1, f32[8,1024]{1,0:T(8,128)} %speed_in.1, f32[8,1024]{1,0:T(8,128)} %dir_in.1, bf16[96,8,1024]{2,1,0:T(8,128)(2,1)} %spectrum.1, ...), custom_call_target="tpu_custom_call" | custom-call | tf_op jit(solution)/shard_map/pallas_call | solution.py:383
  78.6 1.1 %copy.10 = bf16[96,8,1024]{2,1,0:T(8,128)(2,1)} copy(bf16[96,8,1024]{2,1,0:T(8,128)(2,1)S(1)} %shard_map.82) | data formatting | bytes 3145728

commit v5 on v4

--- a/solution.py
+++ b/solution.py
@@ -41,7 +41,7 @@
     tab, table, sea_own, depth_own, wind_speed, wind_dir, block, west, east, near_sea, near_depth, speed, sea, natural, sent, points, couple,
     state, nonlin, rounded, winds, back, turned,
     small_sem, load_sem, couple_sem, mask_send, mask_recv, halo_send, halo_recv,
-    out_send, out_recv, back_send, back_recv, own_sem,
+    out_send, out_recv, back_send, back_recv, own_sem, store_sem,
 ):
     me = lax.axis_index("comp")
     tile = lax.axis_index("tile")
@@ -352,7 +352,8 @@
     def finish(p):
         place(p, 1)
         lanes = pl.ds(pl.multiple_of(p * LANES, LANES), LANES)
-        out[:, :, lanes] = turned[p].reshape(comps, columns, LANES).astype(BF16)
+        block[:, :, lanes] = turned[p].reshape(comps, columns, LANES).astype(BF16)
+        pltpu.make_async_copy(block.at[:, :, lanes], out.at[:, :, lanes], store_sem).start()
 
     own_back(1).wait()
     finish(me)
@@ -364,6 +365,7 @@
         return carry
 
     lax.fori_loop(0, parts - 1, arrived, 0)
+    pltpu.make_async_copy(block, out, store_sem).wait()
 
     for g in range(GROUPS):
         pltpu.make_async_copy(
@@ -384,7 +386,7 @@
         functools.partial(step_kernel, parts, tiles),
         out_shape=jax.ShapeDtypeStruct(spectrum.shape, BF16),
         in_specs=[hbm] * 8,
-        out_specs=pl.BlockSpec(memory_space=pltpu.VMEM),
+        out_specs=hbm,
         scratch_shapes=[
             pltpu.SMEM(tab.shape, F32),
             pltpu.SMEM(group_speed.shape, F32),
@@ -411,7 +413,7 @@
             pltpu.VMEM((parts, comps * 8, LANES), F32),
             dma((6,)), dma((freqs,)), dma,
             dma((2, 2)), dma((2, 2)), dma((4, freqs)), dma((4, freqs)),
-            dma((GROUPS,)), dma((GROUPS,)), dma((GROUPS,)), dma((GROUPS, parts)), dma((2 * GROUPS,)),
+            dma((GROUPS,)), dma((GROUPS,)), dma((GROUPS,)), dma((GROUPS, parts)), dma((2 * GROUPS,)), dma,
         ],
         compiler_params=pltpu.CompilerParams(collective_id=0, has_side_effects=True, vmem_limit_bytes=48 << 20),
     )(*(pltpu.with_memory_space_constraint(a, pltpu.HBM) for a in (tab, group_speed, sea_mask, depth_class, wind_speed, wind_dir, spectrum, coupling)))

time: 79.8 us -> 79.9 us (level)
  no operation moved by 1% of the time
where the time goes in v5:
time: 79.9 us; the launch traced here: 79.8 us
  Pallas kernels  78.6 us (98%)
  local copies, waits for them, and re-layouts  1.15 us (1%)
    pallas_call x1, Pallas kernels, on_device(): pl.pallas_call(functools.partial(step_kernel, parts, tiles), out_shape=ja...  78.6 us

profile of v5, /device:TPU:32, one launch (start us, length us, event | category | flops | bytes accessed | tf_op | source)
XLA Modules:
  0.0 79.8 jit_solution(1859566934671067339)
XLA Ops:
  0.0 78.6 %shard_map.82 = bf16[96,8,1024]{2,1,0:T(8,128)(2,1)S(1)} custom-call(f32[5,32]{1,0:T(8,128)} %constant.2.clone.tab_in, f32[16,32]{1,0:T(8,128)} %table_in.1, s32[8,1024]{1,0:T(8,128)} %sea_in.1, s32[8,1024]{1,0:T(8,128)} %depth_in.1, f32[8,1024]{1,0:T(8,128)} %speed_in.1, f32[8,1024]{1,0:T(8,128)} %dir_in.1, bf16[96,8,1024]{2,1,0:T(8,128)(2,1)} %spectrum.1, ...), custom_call_target="tpu_custom_call" | custom-call | tf_op jit(solution)/shard_map/pallas_call | solution.py:385
  78.6 1.1 %copy.10 = bf16[96,8,1024]{2,1,0:T(8,128)(2,1)} copy(bf16[96,8,1024]{2,1,0:T(8,128)(2,1)S(1)} %shard_map.82) | data formatting | bytes 3145728
